TPU v7x, 32 devices: a whole 2x2x4 slice. The times are simulated.
32 devices in a mesh: wide: 8 (over z, x), narrow: 4 (over y, core).
Axes of the slice: x: 2, y: 2, z: 4, core: 2. Of those that a mesh axis runs over, the one named last changes fastest.
Arguments:
- hidden_in: bfloat16 [16384, 1024], P(('wide', 'narrow')), may hold values from -6 to 6
- grad_out: bfloat16 [16384, 1024], P(('wide', 'narrow')), may hold values from -6 to 6
- gain_attn: bfloat16 [1024], replicated, may hold values from 0.5 to 1.5
- gain_ffn: bfloat16 [1024], replicated, may hold values from 0.5 to 1.5
- w_query: bfloat16 [1024, 1024], P(None, 'narrow'), may hold values from -0.046875 to 0.046875
- w_key: bfloat16 [1024, 1024], P(None, 'narrow'), may hold values from -0.1875 to 0.1875
- w_value: bfloat16 [1024, 1024], P(None, 'narrow'), may hold values from -0.1875 to 0.1875
- w_output: bfloat16 [1024, 1024], P('narrow'), may hold values from -0.75 to 0.75
- table_rel: bfloat16 [32, 16], P(None, 'narrow'), may hold values from -4 to 4
- table_horiz: bfloat16 [32, 16], P(None, 'narrow'), may hold values from -4 to 4
- table_vert: bfloat16 [32, 16], P(None, 'narrow'), may hold values from -4 to 4
- wi_gate: bfloat16 [1024, 2816], P(None, 'narrow'), may hold values from -0.1875 to 0.1875
- wi_up: bfloat16 [1024, 2816], P(None, 'narrow'), may hold values from -0.1875 to 0.1875
- wo_ffn: bfloat16 [2816, 1024], P('narrow'), may hold values from -0.21875 to 0.21875
- counts: int32 [32], P('wide'), may hold values from 1 to 256
- patch_mask: int32 [32, 256], P('wide'), may hold values 0 or 1
- bucket_rel: int32 [32, 512, 512], P('wide'), may hold values from 0 to 31
- bucket_horiz: int32 [32, 512, 512], P('wide'), may hold values from 0 to 31
- bucket_vert: int32 [32, 512, 512], P('wide'), may hold values from 0 to 31
Outputs:
- block_out: bfloat16 [16384, 1024], P(('wide', 'narrow'))
- grad_input: float32 [16384, 1024], P(('wide', 'narrow'))
- grad_gain_attn: float32 [1024], P(('wide', 'narrow'))
- grad_gain_ffn: float32 [1024], P(('wide', 'narrow'))
- grad_w_query: float32 [1024, 1024], P('wide', 'narrow')
- grad_w_key: float32 [1024, 1024], P('wide', 'narrow')
- grad_w_value: float32 [1024, 1024], P('wide', 'narrow')
- grad_w_output: float32 [1024, 1024], P('narrow', 'wide')
- grad_table_rel: float32 [32, 16], P('wide', 'narrow')
- grad_table_horiz: float32 [32, 16], P('wide', 'narrow')
- grad_table_vert: float32 [32, 16], P('wide', 'narrow')
- grad_wi_gate: float32 [1024, 2816], P('wide', 'narrow')
- grad_wi_up: float32 [1024, 2816], P('wide', 'narrow')
- grad_wo_ffn: float32 [2816, 1024], P('narrow', 'wide')
All inputs are finite; a program needn't handle non-finite values. No bound on the sum of `patch_mask` on one device may be relied on, other than what follows from the above.
Results may differ from a plain program's by a relative error of at most 0.02.
Values may be sent and summed in bfloat16 or wider, within the bound.
A program may use at most 256 MiB of HBM per device.

v0:
```python
from functools import partial
import jax
import jax.numpy as jnp
from jax import lax
from jax.sharding import PartitionSpec as P

HEAD_DIM = 64
EPS = 1e-06
MASKED = -1000000000.0


def rms_forward(row_data, gain_vec):
    inv_rms = lax.rsqrt(jnp.mean(row_data * row_data, axis=-1, keepdims=True) + EPS)
    return (row_data * inv_rms * gain_vec, inv_rms)


def rms_backward(upstream, row_data, inv_rms, gain_vec):
    lifted = upstream * gain_vec
    inner = jnp.mean(lifted * row_data, axis=-1, keepdims=True)
    grad_rows = inv_rms * lifted - row_data * inv_rms * inv_rms * inv_rms * inner
    grad_gain = jnp.sum(upstream * row_data * inv_rms, axis=0)
    return (grad_rows, grad_gain)


def bucket_onehot(bucket_rel, bucket_horiz, bucket_vert, buckets):
    levels = jnp.arange(buckets, dtype=jnp.int32)[None, :, None]
    pieces = [
        (bucket_ids[:, None, :] == levels).astype(jnp.bfloat16)
        for bucket_ids in (bucket_rel, bucket_horiz, bucket_vert)
    ]
    return jnp.concatenate(pieces, axis=1)


def page_scores(queries, key_rows, one_hot, table_all, valid):
    scores = jnp.einsum("ihd,jhd->hij", queries, key_rows, preferred_element_type=jnp.float32)
    scores = scores + jnp.einsum(
        "ibj,bh->hij", one_hot, table_all, preferred_element_type=jnp.float32
    )
    return jnp.where(valid[None, None, :], scores, MASKED)


def page_forward(table_all, page_data):
    queries, key_rows, values, bucket_rel, bucket_horiz, bucket_vert, valid = page_data
    one_hot = bucket_onehot(bucket_rel, bucket_horiz, bucket_vert, table_all.shape[0] // 3)
    scores = page_scores(queries, key_rows, one_hot, table_all, valid)
    peak = jnp.max(scores, axis=-1, keepdims=True)
    raised = jnp.exp(scores - peak)
    summed = jnp.sum(raised, axis=-1, keepdims=True)
    weights_low = (raised / summed).astype(jnp.bfloat16)
    context = jnp.einsum("hij,jhd->ihd", weights_low, values, preferred_element_type=jnp.float32)
    return (context.astype(jnp.bfloat16), (peak + jnp.log(summed))[..., 0])


def page_backward(table_all, page_data):
    (
        queries,
        key_rows,
        values,
        grad_context,
        bucket_rel,
        bucket_horiz,
        bucket_vert,
        valid,
        log_total,
    ) = page_data
    one_hot = bucket_onehot(bucket_rel, bucket_horiz, bucket_vert, table_all.shape[0] // 3)
    scores = page_scores(queries, key_rows, one_hot, table_all, valid)
    weights = jnp.exp(scores - log_total[..., None])
    weights_low = weights.astype(jnp.bfloat16)
    grad_values = jnp.einsum(
        "hij,ihd->jhd", weights_low, grad_context, preferred_element_type=jnp.float32
    )
    grad_weights = jnp.einsum(
        "ihd,jhd->hij", grad_context, values, preferred_element_type=jnp.float32
    )
    grad_scores = weights * (grad_weights - jnp.sum(weights * grad_weights, axis=-1, keepdims=True))
    grad_low = grad_scores.astype(jnp.bfloat16)
    grad_queries = jnp.einsum(
        "hij,jhd->ihd", grad_low, key_rows, preferred_element_type=jnp.float32
    )
    grad_keys = jnp.einsum("hij,ihd->jhd", grad_low, queries, preferred_element_type=jnp.float32)
    grad_table = jnp.einsum("ibj,hij->bh", one_hot, grad_low, preferred_element_type=jnp.float32)
    return (
        grad_queries.astype(jnp.bfloat16),
        grad_keys.astype(jnp.bfloat16),
        grad_values.astype(jnp.bfloat16),
        grad_table,
    )


def gated(gate, upper):
    return jax.nn.gelu(gate, approximate=True) * upper


def shards(
    hidden_in,
    grad_out,
    gain_attn,
    gain_ffn,
    w_query,
    w_key,
    w_value,
    w_output,
    table_rel,
    table_horiz,
    table_vert,
    wi_gate,
    wi_up,
    wo_ffn,
    counts,
    patch_mask,
    bucket_rel,
    bucket_horiz,
    bucket_vert,
):
    page_count = bucket_rel.shape[0]
    slot_count = bucket_rel.shape[1]
    local_heads = table_rel.shape[1]
    local_width = w_query.shape[1]
    group_rows = page_count * slot_count
    bucket_count = table_rel.shape[0]
    positions = jnp.arange(slot_count, dtype=jnp.int32)
    text_length = slot_count - patch_mask.shape[1]
    valid = jnp.concatenate(
        [positions[None, :text_length] < counts[:, None], patch_mask == 1], axis=1
    )
    table_all = jnp.concatenate([table_rel, table_horiz, table_vert], axis=0)
    w_joined = jnp.concatenate([w_query, w_key, w_value], axis=1)
    gain_first = gain_attn.astype(jnp.float32)
    gain_second = gain_ffn.astype(jnp.float32)
    resid = hidden_in.astype(jnp.float32)
    normed, inv_first = rms_forward(resid, gain_first)
    normed_all = lax.all_gather(normed.astype(jnp.bfloat16), "narrow", axis=0, tiled=True)
    projected = jnp.dot(normed_all, w_joined, preferred_element_type=jnp.float32).astype(
        jnp.bfloat16
    )
    shaped = projected.reshape(page_count, slot_count, 3, local_heads, HEAD_DIM)
    queries = shaped[:, :, 0]
    key_rows = shaped[:, :, 1]
    values = shaped[:, :, 2]
    context, log_total = lax.map(
        partial(page_forward, table_all),
        (queries, key_rows, values, bucket_rel, bucket_horiz, bucket_vert, valid),
    )
    context_flat = context.reshape(group_rows, local_width)
    middle = resid + lax.psum_scatter(
        jnp.dot(context_flat, w_output, preferred_element_type=jnp.float32),
        "narrow",
        scatter_dimension=0,
        tiled=True,
    )
    normed_ffn, inv_second = rms_forward(middle, gain_second)
    normed_low = normed_ffn.astype(jnp.bfloat16)
    ffn_rows_all = lax.all_gather(normed_low, "narrow", axis=0, tiled=True)
    gate = jnp.dot(ffn_rows_all, wi_gate, preferred_element_type=jnp.float32)
    upper = jnp.dot(ffn_rows_all, wi_up, preferred_element_type=jnp.float32)
    hidden = gated(gate, upper).astype(jnp.bfloat16)
    ffn_out = lax.psum_scatter(
        jnp.dot(hidden, wo_ffn, preferred_element_type=jnp.float32).astype(jnp.bfloat16),
        "narrow",
        scatter_dimension=0,
        tiled=True,
    ).astype(jnp.float32)
    block_out = (middle + ffn_out).astype(jnp.bfloat16)
    grad_resid = grad_out.astype(jnp.float32)
    grad_all = lax.all_gather(grad_out, "narrow", axis=0, tiled=True)
    grad_hidden = jnp.dot(grad_all, wo_ffn.T, preferred_element_type=jnp.float32)
    grad_wo_ffn = jnp.dot(hidden.T, grad_all, preferred_element_type=jnp.float32)
    gated_out, pull = jax.vjp(gated, gate, upper)
    grad_gate, grad_upper = pull(grad_hidden)
    grad_gate = grad_gate.astype(jnp.bfloat16)
    grad_upper = grad_upper.astype(jnp.bfloat16)
    grad_wi_gate = jnp.dot(ffn_rows_all.T, grad_gate, preferred_element_type=jnp.float32)
    grad_wi_up = jnp.dot(ffn_rows_all.T, grad_upper, preferred_element_type=jnp.float32)
    first = jnp.dot(grad_gate, wi_gate.T, preferred_element_type=jnp.float32)
    grad_normed_ffn = lax.psum_scatter(
        first + jnp.dot(grad_upper, wi_up.T, preferred_element_type=jnp.float32),
        "narrow",
        scatter_dimension=0,
        tiled=True,
    )
    grad_middle_norm, grad_gain_second = rms_backward(
        grad_normed_ffn, middle, inv_second, gain_second
    )
    grad_middle = grad_resid + grad_middle_norm
    grad_attn_all = lax.all_gather(grad_middle.astype(jnp.bfloat16), "narrow", axis=0, tiled=True)
    grad_context = jnp.dot(grad_attn_all, w_output.T, preferred_element_type=jnp.float32).astype(
        jnp.bfloat16
    )
    grad_w_output = jnp.dot(context_flat.T, grad_attn_all, preferred_element_type=jnp.float32)
    grad_context_pages = grad_context.reshape(page_count, slot_count, local_heads, HEAD_DIM)
    grad_queries, grad_keys, grad_values, grad_tables = lax.map(
        partial(page_backward, table_all),
        (
            queries,
            key_rows,
            values,
            grad_context_pages,
            bucket_rel,
            bucket_horiz,
            bucket_vert,
            valid,
            log_total,
        ),
    )
    grad_table_all = jnp.sum(grad_tables, axis=0)
    grad_joined = jnp.stack([grad_queries, grad_keys, grad_values], axis=2).reshape(
        group_rows, 3 * local_width
    )
    grad_w_joined = jnp.dot(normed_all.T, grad_joined, preferred_element_type=jnp.float32)
    grad_normed = lax.psum_scatter(
        jnp.dot(grad_joined, w_joined.T, preferred_element_type=jnp.float32).astype(jnp.bfloat16),
        "narrow",
        scatter_dimension=0,
        tiled=True,
    ).astype(jnp.float32)
    grad_resid_norm, grad_gain_first = rms_backward(grad_normed, resid, inv_first, gain_first)
    grad_input = grad_middle + grad_resid_norm
    summed = (
        lax.psum_scatter(
            grad_w_joined[:, :local_width].astype(jnp.bfloat16),
            "wide",
            scatter_dimension=0,
            tiled=True,
        ).astype(jnp.float32),
        lax.psum_scatter(
            grad_w_joined[:, local_width : 2 * local_width].astype(jnp.bfloat16),
            "wide",
            scatter_dimension=0,
            tiled=True,
        ).astype(jnp.float32),
        lax.psum_scatter(
            grad_w_joined[:, 2 * local_width :].astype(jnp.bfloat16),
            "wide",
            scatter_dimension=0,
            tiled=True,
        ).astype(jnp.float32),
        lax.psum_scatter(
            grad_w_output.astype(jnp.bfloat16), "wide", scatter_dimension=1, tiled=True
        ).astype(jnp.float32),
        lax.psum_scatter(
            grad_table_all[:bucket_count].astype(jnp.bfloat16),
            "wide",
            scatter_dimension=0,
            tiled=True,
        ).astype(jnp.float32),
        lax.psum_scatter(
            grad_table_all[bucket_count : 2 * bucket_count].astype(jnp.bfloat16),
            "wide",
            scatter_dimension=0,
            tiled=True,
        ).astype(jnp.float32),
        lax.psum_scatter(
            grad_table_all[2 * bucket_count :].astype(jnp.bfloat16),
            "wide",
            scatter_dimension=0,
            tiled=True,
        ).astype(jnp.float32),
        lax.psum_scatter(
            grad_wi_gate.astype(jnp.bfloat16), "wide", scatter_dimension=0, tiled=True
        ).astype(jnp.float32),
        lax.psum_scatter(
            grad_wi_up.astype(jnp.bfloat16), "wide", scatter_dimension=0, tiled=True
        ).astype(jnp.float32),
        lax.psum_scatter(
            grad_wo_ffn.astype(jnp.bfloat16), "wide", scatter_dimension=1, tiled=True
        ).astype(jnp.float32),
    )
    gain_grads = (
        lax.psum_scatter(grad_gain_first, ("wide", "narrow"), scatter_dimension=0, tiled=True),
        lax.psum_scatter(grad_gain_second, ("wide", "narrow"), scatter_dimension=0, tiled=True),
    )
    return (
        block_out,
        grad_input,
        gain_grads[0],
        gain_grads[1],
        summed[0],
        summed[1],
        summed[2],
        summed[3],
        summed[4],
        summed[5],
        summed[6],
        summed[7],
        summed[8],
        summed[9],
    )


def solution(mesh):
    return jax.shard_map(
        shards,
        mesh=mesh,
        in_specs=(
            P(("wide", "narrow"), None),
            P(("wide", "narrow"), None),
            P(),
            P(),
            P(None, "narrow"),
            P(None, "narrow"),
            P(None, "narrow"),
            P("narrow", None),
            P(None, "narrow"),
            P(None, "narrow"),
            P(None, "narrow"),
            P(None, "narrow"),
            P(None, "narrow"),
            P("narrow", None),
            P("wide"),
            P("wide", None),
            P("wide", None, None),
            P("wide", None, None),
            P("wide", None, None),
        ),
        out_specs=(
            P(("wide", "narrow"), None),
            P(("wide", "narrow"), None),
            P(("wide", "narrow")),
            P(("wide", "narrow")),
            P("wide", "narrow"),
            P("wide", "narrow"),
            P("wide", "narrow"),
            P("narrow", "wide"),
            P("wide", "narrow"),
            P("wide", "narrow"),
            P("wide", "narrow"),
            P("wide", "narrow"),
            P("wide", "narrow"),
            P("narrow", "wide"),
        ),
        check_vma=False,
    )
```

profile of v0, /device:TPU:0, one launch (start us, length us, event | category | flops | bytes accessed | tf_op | source)
XLA Modules:
  0.0 1441.9 jit_solution(14907806034434537034)
XLA Ops:
  15.8 34.4 %all-gather.5.cloned.1.call-done = bf16[2048,1024]{1,0:T(8,128)(2,1)} async-done(((bf16[512,1024]{1,0:T(8,128)(2,1)}), bf16[2048,1024]{1,0:T(8,128)(2,1)}) %all-gather.5.cloned.1.call-update) | async-done | bytes 4194320 | tf_op jit(solution)/shard_map/all_gather | solution.py:133
  76.8 243.5 %while.28 = (s32[]{:T(128)}, bf16[4,512,4,64]{1,3,2,0:T(8,128)(2,1)}, f32[4,4,512]{2,1,0:T(4,128)}, bf16[4,512,4,64]{1,3,2,0:T(8,128)(2,1)}, pred[4,512]{1,0:T(4...) while((s32[]{:T(128)}, ...), condition=%wide.region_4.5_spmd, body=%wide.region_1.4_spmd.sunk | while | flops 553777152 | bytes 90247560 | solution.py:141
  108.1 17.5 %fusion.146 = f32[512,512,4]{1,2,0:T(4,128)} fusion(pred[512,32,512]{2,1,0:T(32,128)(4,1)} %iota_compare_fusion.12, pred[512,32,512]{2,1,0:T(32,128)(4,1)} %iota_compare_fusion.13, pred[512,32,512]{2,1,0:T(32,128)(4,1)} %iota_compare_fusion.14, bf16[96,4]{0,1:T(4,128)(2,1)S(1)} %get-tuple-element.520), kind=kOutput, calls=%fused_computation.1.clone.1 | convolution fusion | flops 251658240 | bytes 29360896 | tf_op jit(solution)/shard_map/while/body/eval_jaxpr/ibj,bh->hij/dot_general | solution.py:36
  168.8 17.5 %fusion.146 = f32[512,512,4]{1,2,0:T(4,128)} fusion(pred[512,32,512]{2,1,0:T(32,128)(4,1)} %iota_compare_fusion.12, pred[512,32,512]{2,1,0:T(32,128)(4,1)} %iota_compare_fusion.13, pred[512,32,512]{2,1,0:T(32,128)(4,1)} %iota_compare_fusion.14, bf16[96,4]{0,1:T(4,128)(2,1)S(1)} %get-tuple-element.520), kind=kOutput, calls=%fused_computation.1.clone.1 | convolution fusion | flops 251658240 | bytes 29360896 | tf_op jit(solution)/shard_map/while/body/eval_jaxpr/ibj,bh->hij/dot_general | solution.py:36
  229.6 17.5 %fusion.146 = f32[512,512,4]{1,2,0:T(4,128)} fusion(pred[512,32,512]{2,1,0:T(32,128)(4,1)} %iota_compare_fusion.12, pred[512,32,512]{2,1,0:T(32,128)(4,1)} %iota_compare_fusion.13, pred[512,32,512]{2,1,0:T(32,128)(4,1)} %iota_compare_fusion.14, bf16[96,4]{0,1:T(4,128)(2,1)S(1)} %get-tuple-element.520), kind=kOutput, calls=%fused_computation.1.clone.1 | convolution fusion | flops 251658240 | bytes 29360896 | tf_op jit(solution)/shard_map/while/body/eval_jaxpr/ibj,bh->hij/dot_general | solution.py:36
  290.3 17.5 %fusion.146 = f32[512,512,4]{1,2,0:T(4,128)} fusion(pred[512,32,512]{2,1,0:T(32,128)(4,1)} %iota_compare_fusion.12, pred[512,32,512]{2,1,0:T(32,128)(4,1)} %iota_compare_fusion.13, pred[512,32,512]{2,1,0:T(32,128)(4,1)} %iota_compare_fusion.14, bf16[96,4]{0,1:T(4,128)(2,1)S(1)} %get-tuple-element.520), kind=kOutput, calls=%fused_computation.1.clone.1 | convolution fusion | flops 251658240 | bytes 29360896 | tf_op jit(solution)/shard_map/while/body/eval_jaxpr/ibj,bh->hij/dot_general | solution.py:36
  328.9 71.2 %reduce-scatter.20.cloned.1.call-done = f32[512,1024]{1,0:T(8,128)} async-done(((f32[2048,1024]{1,0:T(8,128)}), f32[512,1024]{1,0:T(8,128)}) %reduce-scatter.20.cloned.1.call-update) | async-done | bytes 2097168 | tf_op jit(solution)/shard_map/reduce_scatter | solution.py:146
  404.4 34.0 %all-gather.7.cloned.1.call-done = bf16[2048,1024]{1,0:T(8,128)(2,1)} async-done(((bf16[512,1024]{1,0:T(8,128)(2,1)}), bf16[2048,1024]{1,0:T(8,128)(2,1)}) %all-gather.7.cloned.1.call-update) | async-done | bytes 4194320 | tf_op jit(solution)/shard_map/all_gather | solution.py:154
  452.1 22.3 %all-gather.9.cloned.1.call-done = bf16[2048,1024]{1,0:T(8,128)(2,1)} async-done(((bf16[512,1024]{1,0:T(8,128)(2,1)}), bf16[2048,1024]{1,0:T(8,128)(2,1)}) %all-gather.9.cloned.1.call-update) | async-done | bytes 4194320 | tf_op jit(solution)/shard_map/all_gather | solution.py:166
  496.3 71.8 %reduce-scatter.24.cloned.1.call-done = f32[512,1024]{1,0:T(8,128)} async-done(((f32[2048,1024]{1,0:T(8,128)}), f32[512,1024]{1,0:T(8,128)}) %reduce-scatter.24.cloned.1.call-update) | async-done | bytes 2097168 | tf_op jit(solution)/shard_map/reduce_scatter | solution.py:176
  621.3 447.7 %while.29 = (s32[]{:T(128)}, bf16[4,512,4,64]{1,3,2,0:T(8,128)(2,1)}, bf16[4,512,4,64]{1,3,2,0:T(8,128)(2,1)}, bf16[4,512,4,64]{1,3,2,0:T(8,128)(2,1)}, f32[4,96...) while((s32[]{:T(128)}, ...), condition=%wide.region_12.13_spmd, body=%wide.region_10.12_spmd.sunk | while | flops 1159067648 | bytes 209244656 | solution.py:192
  673.7 17.6 %pad_add_fusion.7 = pred[512,96,512]{2,1,0:T(32,128)(4,1)} fusion(pred[512,32,512]{2,1,0:T(32,128)(4,1)} %iota_compare_fusion.15, pred[512,32,512]{2,1,0:T(32,128)(4,1)} %iota_compare_fusion.16, pred[512,32,512]{2,1,0:T(32,128)(4,1)} %iota_compare_fusion.17), kind=kLoop, calls=%fused_computation.29.clone.1 | loop fusion | flops 50331648 | bytes 50331648 | tf_op jit(solution)/shard_map/while/body/eval_jaxpr/concatenate | solution.py:31
  729.3 16.9 %fusion.167 = f32[4,96,4]{1,2,0:T(4,128)} fusion(f32[4,96,4]{1,2,0:T(4,128)} %get-tuple-element.542, s32[]{:T(128)S(6)} %copy.127, pred[512,96,512]{2,1,0:T(32,128)(4,1)} %pad_add_fusion.7, bf16[4,512,512]{2,0,1:T(4,128)(2,1)} %copy.104), kind=kOutput, calls=%fused_computation.51.clone.1 | convolution fusion | flops 201326592 | bytes 27265028 | tf_op jit(solution)/shard_map/while/body/eval_jaxpr/ibj,hij->bh/dot_general | solution.py:82
  781.5 17.7 %pad_add_fusion.7 = pred[512,96,512]{2,1,0:T(32,128)(4,1)} fusion(pred[512,32,512]{2,1,0:T(32,128)(4,1)} %iota_compare_fusion.15, pred[512,32,512]{2,1,0:T(32,128)(4,1)} %iota_compare_fusion.16, pred[512,32,512]{2,1,0:T(32,128)(4,1)} %iota_compare_fusion.17), kind=kLoop, calls=%fused_computation.29.clone.1 | loop fusion | flops 50331648 | bytes 50331648 | tf_op jit(solution)/shard_map/while/body/eval_jaxpr/concatenate | solution.py:31
  837.1 16.7 %fusion.167 = f32[4,96,4]{1,2,0:T(4,128)} fusion(f32[4,96,4]{1,2,0:T(4,128)} %get-tuple-element.542, s32[]{:T(128)S(6)} %copy.127, pred[512,96,512]{2,1,0:T(32,128)(4,1)} %pad_add_fusion.7, bf16[4,512,512]{2,0,1:T(4,128)(2,1)} %copy.104), kind=kOutput, calls=%fused_computation.51.clone.1 | convolution fusion | flops 201326592 | bytes 27265028 | tf_op jit(solution)/shard_map/while/body/eval_jaxpr/ibj,hij->bh/dot_general | solution.py:82
  889.1 17.5 %pad_add_fusion.7 = pred[512,96,512]{2,1,0:T(32,128)(4,1)} fusion(pred[512,32,512]{2,1,0:T(32,128)(4,1)} %iota_compare_fusion.15, pred[512,32,512]{2,1,0:T(32,128)(4,1)} %iota_compare_fusion.16, pred[512,32,512]{2,1,0:T(32,128)(4,1)} %iota_compare_fusion.17), kind=kLoop, calls=%fused_computation.29.clone.1 | loop fusion | flops 50331648 | bytes 50331648 | tf_op jit(solution)/shard_map/while/body/eval_jaxpr/concatenate | solution.py:31
  944.5 16.7 %fusion.167 = f32[4,96,4]{1,2,0:T(4,128)} fusion(f32[4,96,4]{1,2,0:T(4,128)} %get-tuple-element.542, s32[]{:T(128)S(6)} %copy.127, pred[512,96,512]{2,1,0:T(32,128)(4,1)} %pad_add_fusion.7, bf16[4,512,512]{2,0,1:T(4,128)(2,1)} %copy.104), kind=kOutput, calls=%fused_computation.51.clone.1 | convolution fusion | flops 201326592 | bytes 27265028 | tf_op jit(solution)/shard_map/while/body/eval_jaxpr/ibj,hij->bh/dot_general | solution.py:82
  996.6 17.5 %pad_add_fusion.7 = pred[512,96,512]{2,1,0:T(32,128)(4,1)} fusion(pred[512,32,512]{2,1,0:T(32,128)(4,1)} %iota_compare_fusion.15, pred[512,32,512]{2,1,0:T(32,128)(4,1)} %iota_compare_fusion.16, pred[512,32,512]{2,1,0:T(32,128)(4,1)} %iota_compare_fusion.17), kind=kLoop, calls=%fused_computation.29.clone.1 | loop fusion | flops 50331648 | bytes 50331648 | tf_op jit(solution)/shard_map/while/body/eval_jaxpr/concatenate | solution.py:31
  1124.5 38.4 %all-reduce.6 = (bf16[32,4]{1,0:T(8,128)(2,1)}, bf16[32,4]{1,0:T(8,128)(2,1)}, bf16[32,4]{1,0:T(8,128)(2,1)}) all-reduce(bf16[32,4]{1,0:T(8,128)(2,1)} %copy.80, bf16[32,4]{1,0:T(8,128)(2,1)} %copy.81, bf16[32,4]{1,0:T(8,128)(2,1)} %copy.82), channel_id=12, replica_groups=mesh['wide'=8,'narrow'=4] {'wide'}, use_global_device_ids=true, to_apply=%region_24.25.clone | all-reduce | flops 384 | bytes 1536
  1169.8 37.6 %reduce-scatter.28.cloned.1.call-done = bf16[128,256]{1,0:T(8,128)(2,1)} async-done(((bf16[1024,256]{1,0:T(8,128)(2,1)}), bf16[128,256]{1,0:T(8,128)(2,1)}) %reduce-scatter.28.cloned.1.call-update) | async-done | bytes 65552 | tf_op jit(solution)/shard_map/reduce_scatter | solution.py:220
  1208.8 63.0 %reduce-scatter.30.cloned.1.call-done = bf16[128,256]{1,0:T(8,128)(2,1)} async-done(((bf16[1024,256]{1,0:T(8,128)(2,1)}), bf16[128,256]{1,0:T(8,128)(2,1)}) %reduce-scatter.30.cloned.1.call-update) | async-done | bytes 65552 | tf_op jit(solution)/shard_map/reduce_scatter | solution.py:226
  1273.3 63.3 %reduce-scatter.32.cloned.1.call-done = bf16[128,256]{1,0:T(8,128)(2,1)} async-done(((bf16[1024,256]{1,0:T(8,128)(2,1)}), bf16[128,256]{1,0:T(8,128)(2,1)}) %reduce-scatter.32.cloned.1.call-update) | async-done | bytes 65552 | tf_op jit(solution)/shard_map/reduce_scatter | solution.py:232
  1338.1 44.7 %reduce-scatter.26.cloned.1.call-done = bf16[512,1024]{1,0:T(8,128)(2,1)} async-done(((bf16[2048,1024]{1,0:T(8,128)(2,1)}), bf16[512,1024]{1,0:T(8,128)(2,1)}) %reduce-scatter.26.cloned.1.call-update) | async-done | bytes 1048592 | tf_op jit(solution)/shard_map/reduce_scatter | solution.py:211
  1385.8 39.9 %all-reduce.5 = (f32[1024]{0:T(1024)}, f32[1024]{0:T(1024)}) all-reduce(f32[1024]{0:T(1024)} %get-tuple-element.227, f32[1024]{0:T(1024)} %get-tuple-element.225), channel_id=6, replica_groups=mesh['wide'=8,'narrow'=4] {'wide','narrow'}, use_global_device_ids=true, to_apply=%region_16.17.clone | all-reduce | flops 2048 | bytes 16384
  (312 shorter events, 697.2 us)
Async XLA Ops:
  7.2 467.2 %copy-start = (bf16[704,1024]{1,0:T(8,128)(2,1)S(1)}, bf16[704,1024]{1,0:T(8,128)(2,1)}, u32[]{:S(2)}) copy-start(bf16[704,1024]{1,0:T(8,128)(2,1)} %param.36) | copy-start | bytes 4325380
  7.3 42.9 %all-gather.5.cloned.1.call-start = ((), (), s32[]{:S(2)}) async-start(), calls=%async_computation.11 | async-start | bytes 5242880 | tf_op jit(solution)/shard_map/all_gather | solution.py:133
  12.8 387.3 %reduce-scatter.20.cloned.1.call-start = ((), (), s32[]{:S(2)}) async-start(), calls=%async_computation.12 | async-start | bytes 10485760 | tf_op jit(solution)/shard_map/reduce_scatter | solution.py:146
  328.2 110.2 %all-gather.7.cloned.1.call-start = ((), (), s32[]{:S(2)}) async-start(), calls=%async_computation.13 | async-start | bytes 5242880 | tf_op jit(solution)/shard_map/all_gather | solution.py:154
  328.9 242.1 %copy-start.13 = (f32[1024]{0:T(1024)}, f32[1024]{0:T(1024)S(1)}, u32[]{:S(2)}) copy-start(f32[1024]{0:T(1024)S(1)} %convert_element_type.142) | copy-start | bytes 12292
  402.3 168.7 %copy-start.2 = (f32[512,1024]{1,0:T(8,128)}, f32[512,1024]{1,0:T(8,128)S(1)}, u32[]{:S(2)}) copy-start(f32[512,1024]{1,0:T(8,128)S(1)} %get-tuple-element.287) | copy-start | bytes 6291460
  402.3 168.7 %copy-start.17 = (f32[512]{0:T(512)}, f32[512]{0:T(512)S(1)}, u32[]{:S(2)}) copy-start(f32[512]{0:T(512)S(1)} %add_rsqrt_fusion) | copy-start | bytes 6148
  403.8 70.6 %all-gather.9.cloned.1.call-start = ((), (), s32[]{:S(2)}) async-start(), calls=%async_computation.15 | async-start | bytes 5242880 | tf_op jit(solution)/shard_map/all_gather | solution.py:166
  404.4 163.8 %reduce-scatter.24.cloned.1.call-start = ((), (), s32[]{:S(2)}) async-start(), calls=%async_computation.16 | async-start | bytes 10485760 | tf_op jit(solution)/shard_map/reduce_scatter | solution.py:176
  496.3 111.7 %all-gather.11.cloned.1.call-start = ((), (), s32[]{:S(2)}) async-start(), calls=%async_computation.17 | async-start | bytes 5242880 | tf_op jit(solution)/shard_map/all_gather | solution.py:186
  573.3 534.1 %reduce-scatter.40.cloned.1.call-start = ((), (), s32[]{:S(2)}) async-start(), calls=%async_computation.25 | async-start | bytes 1769472
  581.6 529.2 %reduce-scatter.38.cloned.1.call-start = ((), (), s32[]{:S(2)}) async-start(), calls=%async_computation.24 | async-start | bytes 1769472
  590.0 524.2 %reduce-scatter.36.cloned.1.call-start = ((), (), s32[]{:S(2)}) async-start(), calls=%async_computation.23 | async-start | bytes 1769472
  597.9 568.8 %reduce-scatter.34.cloned.1.call-start = ((), (), s32[]{:S(2)}) async-start(), calls=%async_computation.22 | async-start | bytes 589824
  1080.9 126.4 %reduce-scatter.28.cloned.1.call-start = ((), (), s32[]{:S(2)}) async-start(), calls=%async_computation.19 | async-start | bytes 589824 | tf_op jit(solution)/shard_map/reduce_scatter | solution.py:220
  1088.8 183.0 %reduce-scatter.30.cloned.1.call-start = ((), (), s32[]{:S(2)}) async-start(), calls=%async_computation.20 | async-start | bytes 589824 | tf_op jit(solution)/shard_map/reduce_scatter | solution.py:226
  1089.4 247.2 %reduce-scatter.32.cloned.1.call-start = ((), (), s32[]{:S(2)}) async-start(), calls=%async_computation.21 | async-start | bytes 589824 | tf_op jit(solution)/shard_map/reduce_scatter | solution.py:232
  1090.2 292.7 %reduce-scatter.26.cloned.1.call-start = ((), (), s32[]{:S(2)}) async-start(), calls=%async_computation.18 | async-start | bytes 5242880 | tf_op jit(solution)/shard_map/reduce_scatter | solution.py:211
  1098.3 332.2 %reduce-scatter.22.cloned.1.call-start = ((), (), s32[]{:S(2)}) async-start(), calls=%async_computation.14 | async-start | bytes 5242880 | tf_op jit(solution)/shard_map/reduce_scatter | solution.py:158
  1105.3 277.5 %copy-start.16 = (f32[1024]{0:T(1024)S(1)}, f32[1024]{0:T(1024)}, u32[]{:S(2)}) copy-start(f32[1024]{0:T(1024)} %copy-done.15) | copy-start | bytes 12292
  1105.3 277.5 %copy-start.22 = (f32[512]{0:T(512)S(1)}, f32[512]{0:T(512)}, u32[]{:S(2)}) copy-start(f32[512]{0:T(512)} %copy-done.21) | copy-start | bytes 6148
  1105.3 325.1 %copy-start.3 = (f32[512,1024]{1,0:T(8,128)S(1)}, f32[512,1024]{1,0:T(8,128)}, u32[]{:S(2)}) copy-start(f32[512,1024]{1,0:T(8,128)} %copy-done.2) | copy-start | bytes 6291460
  1105.3 325.1 %copy-start.14 = (f32[1024]{0:T(1024)S(1)}, f32[1024]{0:T(1024)}, u32[]{:S(2)}) copy-start(f32[1024]{0:T(1024)} %copy-done.13) | copy-start | bytes 12292
  1105.3 325.1 %copy-start.18 = (f32[512]{0:T(512)S(1)}, f32[512]{0:T(512)}, u32[]{:S(2)}) copy-start(f32[512]{0:T(512)} %copy-done.17) | copy-start | bytes 6148
  (33 other events, 218.6 us)
Sparse Core Ops, SparseCore 0:
  12.9 37.1 all-gather.4
  328.3 71.7 reduce-scatter.19
  403.9 34.4 all-gather.6
  439.9 34.4 all-gather.8
  496.4 71.6 reduce-scatter.23
  573.4 34.4 all-gather.10
  611.3 64.8 reduce-scatter.39
  680.0 63.7 reduce-scatter.37
  747.3 63.6 reduce-scatter.35
  1081.0 61.9 reduce-scatter.33
  1146.3 60.9 reduce-scatter.27
  1210.9 60.8 reduce-scatter.29
  1275.7 60.8 reduce-scatter.31
  1339.2 43.5 reduce-scatter.25
  1385.2 45.1 reduce-scatter.21
where the time goes:
time: 1450 us; the launch traced here: 1440 us
  waiting for transfers between devices  455 us (31%)
  matrix products  386 us (27%)
  other arithmetic  335 us (23%)
  local copies, waits for them, and re-layouts  153 us (11%)
  blocking collectives  78.3 us (5%)
  loops' own time  18.1 us (1%)
  between operations  15.2 us (1%)
    eq x24, other arithmetic, bucket_onehot(): bucket_ids[:, None, :] == levels  215 us
    dot_general x8, matrix products, page_scores(): jnp.einsum('ibj,bh->hij', one_hot, table_all, preferred_element_type=jnp....  134 us
    unnamed x2, blocking collectives  78.3 us
    reduce_scatter x1, waiting for transfers between devices, shards(): lax.psum_scatter(first + jnp.dot(grad_upper, wi_up.T, preferred_element_t...  71.8 us
    reduce_scatter x1, waiting for transfers between devices, shards(): lax.psum_scatter(jnp.dot(context_flat, w_output, preferred_element_type=j...  71.2 us
    concatenate x4, other arithmetic, bucket_onehot(): return jnp.concatenate(pieces, axis=1)  70.4 us
    dot_general x4, matrix products, page_backward(): jnp.einsum('ibj,hij->bh', one_hot, grad_low, preferred_element_type=jnp.f...  67 us
    reduce_scatter x1, waiting for transfers between devices, shards(): lax.psum_scatter(grad_w_joined[:, 2 * local_width:].astype(jnp.bfloat16),...  63.3 us
  transfers between devices with their start and end apart: 15, of which 11 were waited for; matrix products, arithmetic and copies ran while one was open for 38% of the time, Pallas kernels for 0%

commit v1 on v0

--- a/solution.py
+++ b/solution.py
@@ -130,7 +130,25 @@
     gain_second = gain_ffn.astype(jnp.float32)
     resid = hidden_in.astype(jnp.float32)
     normed, inv_first = rms_forward(resid, gain_first)
-    normed_all = lax.all_gather(normed.astype(jnp.bfloat16), "narrow", axis=0, tiled=True)
+    array = normed.astype(jnp.bfloat16)
+    size, position, rows = (lax.axis_size("narrow"), lax.axis_index("narrow"), array.shape[0])
+    right = [(i, (i + 1) % size) for i in range(size)]
+    left = [(i, (i - 1) % size) for i in range(size)]
+    out = jnp.zeros((*array.shape[:0], size * rows, *array.shape[0 + 1 :]), array.dtype)
+    out = lax.dynamic_update_slice_in_dim(out, array, position * rows, axis=0)
+    from_left = from_right = array
+    middle_2 = size // 2
+    for hop in range(1, middle_2 + 1):
+        from_left = lax.ppermute(from_left, "narrow", right)
+        out = lax.dynamic_update_slice_in_dim(
+            out, from_left, (position - hop) % size * rows, axis=0
+        )
+        if hop < size - middle_2:
+            from_right = lax.ppermute(from_right, "narrow", left)
+            out = lax.dynamic_update_slice_in_dim(
+                out, from_right, (position + hop) % size * rows, axis=0
+            )
+    normed_all = out
     projected = jnp.dot(normed_all, w_joined, preferred_element_type=jnp.float32).astype(
         jnp.bfloat16
     )

time: 1450 us -> 1480 us (1.021)
  loops' own time: 18.1 us -> 38.6 us
    all_gather x1 -> x0, waiting for transfers between devices: 34.4 us -> none  [shards(): lax.all_gather(normed.astype(jnp.bfloat16), 'narrow', axis=0, tiled=True)]
    ppermute x0 -> x3, waiting for transfers between devices: none -> 25.8 us  [the longest x2 25.8 us: shards(): from_left = lax.ppermute(from_left, 'narrow', right)]
  transfers between devices with their start and end apart: 15 -> 17, of which waited for: 11 -> 12; matrix products, arithmetic and copies ran while one was open for 38% -> 38% of each run, Pallas kernels for 0% -> 0%
where the time goes in v1:
time: 1480 us; the launch traced here: 1470 us
  waiting for transfers between devices  451 us (30%)
  matrix products  385 us (26%)
  other arithmetic  335 us (23%)
  local copies, waits for them, and re-layouts  159 us (11%)
  blocking collectives  78.4 us (5%)
  loops' own time  38.6 us (3%)
  between operations  15.2 us (1%)
    eq x24, other arithmetic, bucket_onehot(): bucket_ids[:, None, :] == levels  215 us
    dot_general x8, matrix products, page_scores(): jnp.einsum('ibj,bh->hij', one_hot, table_all, preferred_element_type=jnp....  134 us
    unnamed x2, blocking collectives  78.4 us
    reduce_scatter x1, waiting for transfers between devices, shards(): lax.psum_scatter(jnp.dot(context_flat, w_output, preferred_element_type=j...  75.2 us
    reduce_scatter x1, waiting for transfers between devices, shards(): lax.psum_scatter(first + jnp.dot(grad_upper, wi_up.T, preferred_element_t...  71.8 us
    concatenate x4, other arithmetic, bucket_onehot(): return jnp.concatenate(pieces, axis=1)  70.6 us
    dot_general x4, matrix products, page_backward(): jnp.einsum('ibj,hij->bh', one_hot, grad_low, preferred_element_type=jnp.f...  67 us
    reduce_scatter x1, waiting for transfers between devices, shards(): lax.psum_scatter(grad_w_joined[:, 2 * local_width:].astype(jnp.bfloat16),...  63.2 us
  transfers between devices with their start and end apart: 17, of which 12 were waited for; matrix products, arithmetic and copies ran while one was open for 38% of the time, Pallas kernels for 0%

profile of v1, /device:TPU:0, one launch (start us, length us, event | category | flops | bytes accessed | tf_op | source)
XLA Modules:
  0.0 1468.8 jit_solution(17675420270767965088)
XLA Ops:
  15.9 21.2 %collective-permute-done = bf16[512,1024]{1,0:T(8,128)(2,1)S(1)} collective-permute-done((bf16[512,1024]{1,0:T(8,128)(2,1)}, bf16[512,1024]{1,0:T(8,128)(2,1)S(1)}, u32[]{:S(2)}, u32[]{:S(2)}) %collective-permute-start) | collective-permute-done | bytes 1048608 | tf_op jit(solution)/shard_map/ppermute | solution.py:142
  78.4 256.5 %while.28 = (s32[]{:T(128)}, bf16[4,512,4,64]{1,3,2,0:T(8,128)(2,1)}, f32[4,4,512]{2,1,0:T(4,128)}, bf16[4,512,4,64]{1,3,2,0:T(8,128)(2,1)}, pred[4,512]{1,0:T(4...) while((s32[]{:T(128)}, ...), condition=%wide.region_4.5_spmd, body=%wide.region_1.4_spmd.sunk | while | flops 553777152 | bytes 90247560 | solution.py:159
  122.5 17.5 %fusion.147 = f32[512,512,4]{1,2,0:T(4,128)} fusion(pred[512,32,512]{2,1,0:T(32,128)(4,1)} %iota_compare_fusion.12, pred[512,32,512]{2,1,0:T(32,128)(4,1)} %iota_compare_fusion.13, pred[512,32,512]{2,1,0:T(32,128)(4,1)} %iota_compare_fusion.14, bf16[96,4]{0,1:T(4,128)(2,1)S(1)} %get-tuple-element.522), kind=kOutput, calls=%fused_computation.1.clone.1 | convolution fusion | flops 251658240 | bytes 29360896 | tf_op jit(solution)/shard_map/while/body/eval_jaxpr/ibj,bh->hij/dot_general | solution.py:36
  183.2 17.5 %fusion.147 = f32[512,512,4]{1,2,0:T(4,128)} fusion(pred[512,32,512]{2,1,0:T(32,128)(4,1)} %iota_compare_fusion.12, pred[512,32,512]{2,1,0:T(32,128)(4,1)} %iota_compare_fusion.13, pred[512,32,512]{2,1,0:T(32,128)(4,1)} %iota_compare_fusion.14, bf16[96,4]{0,1:T(4,128)(2,1)S(1)} %get-tuple-element.522), kind=kOutput, calls=%fused_computation.1.clone.1 | convolution fusion | flops 251658240 | bytes 29360896 | tf_op jit(solution)/shard_map/while/body/eval_jaxpr/ibj,bh->hij/dot_general | solution.py:36
  243.9 17.5 %fusion.147 = f32[512,512,4]{1,2,0:T(4,128)} fusion(pred[512,32,512]{2,1,0:T(32,128)(4,1)} %iota_compare_fusion.12, pred[512,32,512]{2,1,0:T(32,128)(4,1)} %iota_compare_fusion.13, pred[512,32,512]{2,1,0:T(32,128)(4,1)} %iota_compare_fusion.14, bf16[96,4]{0,1:T(4,128)(2,1)S(1)} %get-tuple-element.522), kind=kOutput, calls=%fused_computation.1.clone.1 | convolution fusion | flops 251658240 | bytes 29360896 | tf_op jit(solution)/shard_map/while/body/eval_jaxpr/ibj,bh->hij/dot_general | solution.py:36
  304.7 17.5 %fusion.147 = f32[512,512,4]{1,2,0:T(4,128)} fusion(pred[512,32,512]{2,1,0:T(32,128)(4,1)} %iota_compare_fusion.12, pred[512,32,512]{2,1,0:T(32,128)(4,1)} %iota_compare_fusion.13, pred[512,32,512]{2,1,0:T(32,128)(4,1)} %iota_compare_fusion.14, bf16[96,4]{0,1:T(4,128)(2,1)S(1)} %get-tuple-element.522), kind=kOutput, calls=%fused_computation.1.clone.1 | convolution fusion | flops 251658240 | bytes 29360896 | tf_op jit(solution)/shard_map/while/body/eval_jaxpr/ibj,bh->hij/dot_general | solution.py:36
  343.5 75.2 %reduce-scatter.20.cloned.1.call-done = f32[512,1024]{1,0:T(8,128)} async-done(((f32[2048,1024]{1,0:T(8,128)}), f32[512,1024]{1,0:T(8,128)}) %reduce-scatter.20.cloned.1.call-update) | async-done | bytes 2097168 | tf_op jit(solution)/shard_map/reduce_scatter | solution.py:164
  423.1 33.8 %all-gather.4.cloned.1.call-done = bf16[2048,1024]{1,0:T(8,128)(2,1)} async-done(((bf16[512,1024]{1,0:T(8,128)(2,1)}), bf16[2048,1024]{1,0:T(8,128)(2,1)}) %all-gather.4.cloned.1.call-update) | async-done | bytes 4194320 | tf_op jit(solution)/shard_map/all_gather | solution.py:172
  470.7 22.4 %all-gather.6.cloned.1.call-done = bf16[2048,1024]{1,0:T(8,128)(2,1)} async-done(((bf16[512,1024]{1,0:T(8,128)(2,1)}), bf16[2048,1024]{1,0:T(8,128)(2,1)}) %all-gather.6.cloned.1.call-update) | async-done | bytes 4194320 | tf_op jit(solution)/shard_map/all_gather | solution.py:184
  515.0 71.8 %reduce-scatter.24.cloned.1.call-done = f32[512,1024]{1,0:T(8,128)} async-done(((f32[2048,1024]{1,0:T(8,128)}), f32[512,1024]{1,0:T(8,128)}) %reduce-scatter.24.cloned.1.call-update) | async-done | bytes 2097168 | tf_op jit(solution)/shard_map/reduce_scatter | solution.py:194
  640.1 455.9 %while.29 = (s32[]{:T(128)}, bf16[4,512,4,64]{1,3,2,0:T(8,128)(2,1)}, bf16[4,512,4,64]{1,3,2,0:T(8,128)(2,1)}, bf16[4,512,4,64]{1,3,2,0:T(8,128)(2,1)}, f32[4,96...) while((s32[]{:T(128)}, ...), condition=%wide.region_12.13_spmd, body=%wide.region_10.12_spmd.sunk | while | flops 1159067648 | bytes 209244656 | solution.py:210
  692.5 17.7 %pad_add_fusion.7 = pred[512,96,512]{2,1,0:T(32,128)(4,1)} fusion(pred[512,32,512]{2,1,0:T(32,128)(4,1)} %iota_compare_fusion.15, pred[512,32,512]{2,1,0:T(32,128)(4,1)} %iota_compare_fusion.16, pred[512,32,512]{2,1,0:T(32,128)(4,1)} %iota_compare_fusion.17), kind=kLoop, calls=%fused_computation.29.clone.1 | loop fusion | flops 50331648 | bytes 50331648 | tf_op jit(solution)/shard_map/while/body/eval_jaxpr/concatenate | solution.py:31
  748.2 16.8 %fusion.168 = f32[4,96,4]{1,2,0:T(4,128)} fusion(f32[4,96,4]{1,2,0:T(4,128)} %get-tuple-element.544, s32[]{:T(128)S(6)} %copy.131, pred[512,96,512]{2,1,0:T(32,128)(4,1)} %pad_add_fusion.7, bf16[4,512,512]{2,0,1:T(4,128)(2,1)} %copy.104), kind=kOutput, calls=%fused_computation.51.clone.1 | convolution fusion | flops 201326592 | bytes 27265028 | tf_op jit(solution)/shard_map/while/body/eval_jaxpr/ibj,hij->bh/dot_general | solution.py:82
  800.5 17.8 %pad_add_fusion.7 = pred[512,96,512]{2,1,0:T(32,128)(4,1)} fusion(pred[512,32,512]{2,1,0:T(32,128)(4,1)} %iota_compare_fusion.15, pred[512,32,512]{2,1,0:T(32,128)(4,1)} %iota_compare_fusion.16, pred[512,32,512]{2,1,0:T(32,128)(4,1)} %iota_compare_fusion.17), kind=kLoop, calls=%fused_computation.29.clone.1 | loop fusion | flops 50331648 | bytes 50331648 | tf_op jit(solution)/shard_map/while/body/eval_jaxpr/concatenate | solution.py:31
  856.2 16.7 %fusion.168 = f32[4,96,4]{1,2,0:T(4,128)} fusion(f32[4,96,4]{1,2,0:T(4,128)} %get-tuple-element.544, s32[]{:T(128)S(6)} %copy.131, pred[512,96,512]{2,1,0:T(32,128)(4,1)} %pad_add_fusion.7, bf16[4,512,512]{2,0,1:T(4,128)(2,1)} %copy.104), kind=kOutput, calls=%fused_computation.51.clone.1 | convolution fusion | flops 201326592 | bytes 27265028 | tf_op jit(solution)/shard_map/while/body/eval_jaxpr/ibj,hij->bh/dot_general | solution.py:82
  908.4 17.5 %pad_add_fusion.7 = pred[512,96,512]{2,1,0:T(32,128)(4,1)} fusion(pred[512,32,512]{2,1,0:T(32,128)(4,1)} %iota_compare_fusion.15, pred[512,32,512]{2,1,0:T(32,128)(4,1)} %iota_compare_fusion.16, pred[512,32,512]{2,1,0:T(32,128)(4,1)} %iota_compare_fusion.17), kind=kLoop, calls=%fused_computation.29.clone.1 | loop fusion | flops 50331648 | bytes 50331648 | tf_op jit(solution)/shard_map/while/body/eval_jaxpr/concatenate | solution.py:31
  1015.9 17.5 %pad_add_fusion.7 = pred[512,96,512]{2,1,0:T(32,128)(4,1)} fusion(pred[512,32,512]{2,1,0:T(32,128)(4,1)} %iota_compare_fusion.15, pred[512,32,512]{2,1,0:T(32,128)(4,1)} %iota_compare_fusion.16, pred[512,32,512]{2,1,0:T(32,128)(4,1)} %iota_compare_fusion.17), kind=kLoop, calls=%fused_computation.29.clone.1 | loop fusion | flops 50331648 | bytes 50331648 | tf_op jit(solution)/shard_map/while/body/eval_jaxpr/concatenate | solution.py:31
  1071.4 16.7 %fusion.168 = f32[4,96,4]{1,2,0:T(4,128)} fusion(f32[4,96,4]{1,2,0:T(4,128)} %get-tuple-element.544, s32[]{:T(128)S(6)} %copy.131, pred[512,96,512]{2,1,0:T(32,128)(4,1)} %pad_add_fusion.7, bf16[4,512,512]{2,0,1:T(4,128)(2,1)} %copy.104), kind=kOutput, calls=%fused_computation.51.clone.1 | convolution fusion | flops 201326592 | bytes 27265028 | tf_op jit(solution)/shard_map/while/body/eval_jaxpr/ibj,hij->bh/dot_general | solution.py:82
  1150.7 38.5 %all-reduce.6 = (bf16[32,4]{1,0:T(8,128)(2,1)}, bf16[32,4]{1,0:T(8,128)(2,1)}, bf16[32,4]{1,0:T(8,128)(2,1)}) all-reduce(bf16[32,4]{1,0:T(8,128)(2,1)} %copy.80, bf16[32,4]{1,0:T(8,128)(2,1)} %copy.81, bf16[32,4]{1,0:T(8,128)(2,1)} %copy.82), channel_id=12, replica_groups=mesh['wide'=8,'narrow'=4] {'wide'}, use_global_device_ids=true, to_apply=%region_24.25.clone | all-reduce | flops 384 | bytes 1536
  1196.0 38.0 %reduce-scatter.28.cloned.1.call-done = bf16[128,256]{1,0:T(8,128)(2,1)} async-done(((bf16[1024,256]{1,0:T(8,128)(2,1)}), bf16[128,256]{1,0:T(8,128)(2,1)}) %reduce-scatter.28.cloned.1.call-update) | async-done | bytes 65552 | tf_op jit(solution)/shard_map/reduce_scatter | solution.py:238
  1235.5 63.1 %reduce-scatter.30.cloned.1.call-done = bf16[128,256]{1,0:T(8,128)(2,1)} async-done(((bf16[1024,256]{1,0:T(8,128)(2,1)}), bf16[128,256]{1,0:T(8,128)(2,1)}) %reduce-scatter.30.cloned.1.call-update) | async-done | bytes 65552 | tf_op jit(solution)/shard_map/reduce_scatter | solution.py:244
  1300.2 63.2 %reduce-scatter.32.cloned.1.call-done = bf16[128,256]{1,0:T(8,128)(2,1)} async-done(((bf16[1024,256]{1,0:T(8,128)(2,1)}), bf16[128,256]{1,0:T(8,128)(2,1)}) %reduce-scatter.32.cloned.1.call-update) | async-done | bytes 65552 | tf_op jit(solution)/shard_map/reduce_scatter | solution.py:250
  1364.9 44.7 %reduce-scatter.26.cloned.1.call-done = bf16[512,1024]{1,0:T(8,128)(2,1)} async-done(((bf16[2048,1024]{1,0:T(8,128)(2,1)}), bf16[512,1024]{1,0:T(8,128)(2,1)}) %reduce-scatter.26.cloned.1.call-update) | async-done | bytes 1048592 | tf_op jit(solution)/shard_map/reduce_scatter | solution.py:229
  1412.6 39.9 %all-reduce.5 = (f32[1024]{0:T(1024)}, f32[1024]{0:T(1024)}) all-reduce(f32[1024]{0:T(1024)} %get-tuple-element.227, f32[1024]{0:T(1024)} %get-tuple-element.225), channel_id=6, replica_groups=mesh['wide'=8,'narrow'=4] {'wide','narrow'}, use_global_device_ids=true, to_apply=%region_16.17.clone | all-reduce | flops 2048 | bytes 16384
  (315 shorter events, 712.1 us)
Async XLA Ops:
  7.2 486.0 %copy-start = (bf16[704,1024]{1,0:T(8,128)(2,1)S(1)}, bf16[704,1024]{1,0:T(8,128)(2,1)}, u32[]{:S(2)}) copy-start(bf16[704,1024]{1,0:T(8,128)(2,1)} %param.36) | copy-start | bytes 4325380
  7.2 411.5 %reduce-scatter.20.cloned.1.call-start = ((), (), s32[]{:S(2)}) async-start(), calls=%async_computation.11 | async-start | bytes 10485760 | tf_op jit(solution)/shard_map/reduce_scatter | solution.py:164
  13.4 23.7 %collective-permute-start = (bf16[512,1024]{1,0:T(8,128)(2,1)}, bf16[512,1024]{1,0:T(8,128)(2,1)S(1)}, u32[]{:S(2)}, u32[]{:S(2)}) collective-permute-start(bf16[512,1024]{1,0:T(8,128)(2,1)} %get-tuple-element.289), channel_id=1, source_target_pairs={{0,1},{1,2},{2,3},{3,0},{4,5},{5,6},{6,7},{7,4},{8,9},{9,10},{10,1... | collective-permute-start | bytes 3145736 | tf_op jit(solution)/shard_map/ppermute | solution.py:142
  13.9 31.8 %collective-permute-start.1 = (bf16[512,1024]{1,0:T(8,128)(2,1)}, bf16[512,1024]{1,0:T(8,128)(2,1)S(1)}, u32[]{:S(2)}, u32[]{:S(2)}) collective-permute-start(bf16[512,1024]{1,0:T(8,128)(2,1)} %get-tuple-element.289), channel_id=1, source_target_pairs={{0,3},{1,0},{2,1},{3,2},{4,7},{5,4},{6,5},{7,6},{8,11},{9,8},{10,9... | collective-permute-start | bytes 3145736 | tf_op jit(solution)/shard_map/ppermute | solution.py:147
  37.1 14.2 collective-permute-start.2
  342.9 114.1 %all-gather.4.cloned.1.call-start = ((), (), s32[]{:S(2)}) async-start(), calls=%async_computation.12 | async-start | bytes 5242880 | tf_op jit(solution)/shard_map/all_gather | solution.py:172
  343.5 246.2 %copy-start.14 = (f32[1024]{0:T(1024)}, f32[1024]{0:T(1024)S(1)}, u32[]{:S(2)}) copy-start(f32[1024]{0:T(1024)S(1)} %convert_element_type.142) | copy-start | bytes 12292
  422.4 70.8 %all-gather.6.cloned.1.call-start = ((), (), s32[]{:S(2)}) async-start(), calls=%async_computation.14 | async-start | bytes 5242880 | tf_op jit(solution)/shard_map/all_gather | solution.py:184
  423.1 163.8 %reduce-scatter.24.cloned.1.call-start = ((), (), s32[]{:S(2)}) async-start(), calls=%async_computation.15 | async-start | bytes 10485760 | tf_op jit(solution)/shard_map/reduce_scatter | solution.py:194
  515.0 111.7 %all-gather.8.cloned.1.call-start = ((), (), s32[]{:S(2)}) async-start(), calls=%async_computation.16 | async-start | bytes 5242880 | tf_op jit(solution)/shard_map/all_gather | solution.py:204
  592.0 541.6 %reduce-scatter.40.cloned.1.call-start = ((), (), s32[]{:S(2)}) async-start(), calls=%async_computation.24 | async-start | bytes 1769472
  600.2 536.8 %reduce-scatter.38.cloned.1.call-start = ((), (), s32[]{:S(2)}) async-start(), calls=%async_computation.23 | async-start | bytes 1769472
  608.7 531.8 %reduce-scatter.36.cloned.1.call-start = ((), (), s32[]{:S(2)}) async-start(), calls=%async_computation.22 | async-start | bytes 1769472
  616.6 576.3 %reduce-scatter.34.cloned.1.call-start = ((), (), s32[]{:S(2)}) async-start(), calls=%async_computation.21 | async-start | bytes 589824
  1107.9 126.2 %reduce-scatter.28.cloned.1.call-start = ((), (), s32[]{:S(2)}) async-start(), calls=%async_computation.18 | async-start | bytes 589824 | tf_op jit(solution)/shard_map/reduce_scatter | solution.py:238
  1115.8 182.9 %reduce-scatter.30.cloned.1.call-start = ((), (), s32[]{:S(2)}) async-start(), calls=%async_computation.19 | async-start | bytes 589824 | tf_op jit(solution)/shard_map/reduce_scatter | solution.py:244
  1116.6 246.8 %reduce-scatter.32.cloned.1.call-start = ((), (), s32[]{:S(2)}) async-start(), calls=%async_computation.20 | async-start | bytes 589824 | tf_op jit(solution)/shard_map/reduce_scatter | solution.py:250
  1117.1 292.5 %reduce-scatter.26.cloned.1.call-start = ((), (), s32[]{:S(2)}) async-start(), calls=%async_computation.17 | async-start | bytes 5242880 | tf_op jit(solution)/shard_map/reduce_scatter | solution.py:229
  1124.3 333.0 %reduce-scatter.22.cloned.1.call-start = ((), (), s32[]{:S(2)}) async-start(), calls=%async_computation.13 | async-start | bytes 5242880 | tf_op jit(solution)/shard_map/reduce_scatter | solution.py:176
  1131.5 278.1 %copy-start.17 = (f32[1024]{0:T(1024)S(1)}, f32[1024]{0:T(1024)}, u32[]{:S(2)}) copy-start(f32[1024]{0:T(1024)} %copy-done.16) | copy-start | bytes 12292
  1131.5 278.1 %copy-start.23 = (f32[512]{0:T(512)S(1)}, f32[512]{0:T(512)}, u32[]{:S(2)}) copy-start(f32[512]{0:T(512)} %copy-done.22) | copy-start | bytes 6148
  1131.5 325.8 %copy-start.3 = (f32[512,1024]{1,0:T(8,128)S(1)}, f32[512,1024]{1,0:T(8,128)}, u32[]{:S(2)}) copy-start(f32[512,1024]{1,0:T(8,128)} %copy-done.2) | copy-start | bytes 6291460
  1131.5 325.8 %copy-start.15 = (f32[1024]{0:T(1024)S(1)}, f32[1024]{0:T(1024)}, u32[]{:S(2)}) copy-start(f32[1024]{0:T(1024)} %copy-done.14) | copy-start | bytes 12292
  1131.5 325.8 %copy-start.19 = (f32[512]{0:T(512)S(1)}, f32[512]{0:T(512)}, u32[]{:S(2)}) copy-start(f32[512]{0:T(512)} %copy-done.18) | copy-start | bytes 6148
  (33 other events, 595.8 us)
Sparse Core Ops, SparseCore 0:
  343.0 75.6 reduce-scatter.19
  422.5 34.4 all-gather.3
  458.6 34.4 all-gather.5
  515.1 71.7 reduce-scatter.23
  592.1 34.4 all-gather.7
  629.9 64.8 reduce-scatter.39
  698.6 63.7 reduce-scatter.37
  765.9 63.8 reduce-scatter.35
  1108.0 61.8 reduce-scatter.33
  1173.1 60.8 reduce-scatter.27
  1237.7 60.8 reduce-scatter.29
  1302.5 60.8 reduce-scatter.31
  1366.1 43.5 reduce-scatter.25
  1412.0 45.2 reduce-scatter.21
